TPU v7x, 256 devices: a whole 4x4x8 slice. The times are simulated.
256 devices in a mesh: img: 64 (over y, z_lo, x, core), slab: 4 (over z_hi).
Axes of the slice: x: 4, y: 4, z: 8 (z_hi: 4, z_lo: 2; z = z_hi * 2 + z_lo), core: 2. Of those that a mesh axis runs over, the one named last changes fastest.
Arguments:
- images: bfloat16 [4096, 32768], P('img'), may hold values from -6 to 6
- references: bfloat16 [2, 128, 32768], P(None, 'slab'), may hold values from -6 to 6
- orientations: int32 [4096, 2, 64], P('img'), may hold values from 0 to 127
- ctf_table: float32 [4096, 64], P('img'), may hold values from -1 to 1
- inv_noise: float32 [4096], P('img'), may hold values from 0.002 to 0.02
- class_weight: float32 [2], replicated, may hold values from 0.2 to 5
Outputs:
- updated_volume: float32 [2, 128, 32768], P(None, 'slab', 'img')
All inputs are finite; a program needn't handle non-finite values.
Results may differ from a plain program's by a relative error of at most 0.0065.
Values sent between devices are 32-bit elements; how exact they have to be, the bound alone decides.
A program may use at most 192 MiB of HBM per device.

v0:
```python
import jax
import jax.numpy as jnp
from jax import lax
from jax.sharding import PartitionSpec as P

BOX = 128
SHELLS = 64


def shell_index():
    position = jnp.arange(BOX * BOX, dtype=jnp.int32)
    column = position % BOX - BOX // 2
    row_place = position // BOX - BOX // 2
    radius_sq = column * column + row_place * row_place
    levels = jnp.arange(1, SHELLS, dtype=jnp.int32)
    inside = (2 * levels[None, :] * levels[None, :] <= radius_sq[:, None]).astype(jnp.int32)
    return jnp.sum(inside, axis=1)


def contract_first(left, right):
    return lax.dot_general(
        left, right, (((0,), (0,)), ((), ())), preferred_element_type=jnp.float32
    )


def contract_last(left, right):
    return lax.dot_general(
        left, right, (((1,), (1,)), ((), ())), preferred_element_type=jnp.float32
    )


def shards(images, references, orientations, ctf_table, inv_noise, class_weight):
    batch = images.shape[0]
    classes, local_planes, width = references.shape
    pixels = width // 2
    levels = jnp.arange(SHELLS, dtype=jnp.int32)
    selector = (shell_index()[None, :] == levels[:, None]).astype(jnp.float32)
    ctf_pixel = jnp.dot(
        ctf_table, selector, precision=lax.Precision.HIGHEST, preferred_element_type=jnp.float32
    )
    weighted = (images.astype(jnp.float32) * jnp.repeat(ctf_pixel, 2, axis=1)).astype(jnp.bfloat16)
    ctf_square = (ctf_pixel * ctf_pixel).astype(jnp.bfloat16)
    planes = references.reshape(classes * local_planes, width)
    spread = references.astype(jnp.float32).reshape(classes * local_planes, pixels, 2)
    power = jnp.sum(spread * spread, axis=2).astype(jnp.bfloat16)
    intersection = contract_last(weighted, planes)
    energy = contract_last(ctf_square, power)
    local_table = (2.0 * intersection - energy).reshape(batch, classes, local_planes)
    offset = lax.axis_index("slab") * local_planes
    relative = orientations - offset
    inside = (relative >= 0) & (relative < local_planes)
    prior = jnp.log(class_weight)[None, :, None]
    table = lax.all_gather(local_table, "slab", axis=2, tiled=True)
    picked = jnp.take_along_axis(table, orientations, axis=2)
    scores = prior + inv_noise[:, None, None] * picked
    peak = jnp.max(scores, axis=(1, 2), keepdims=True)
    expo = jnp.exp(scores - peak)
    resp = expo / jnp.sum(expo, axis=(1, 2), keepdims=True)
    local_resp = jnp.where(inside, resp, 0.0)
    plane_ids = jnp.arange(local_planes, dtype=jnp.int32)
    hits = (relative[:, :, :, None] == plane_ids[None, None, None, :]).astype(jnp.float32)
    per_plane = jnp.einsum("bkl,bklp->bkp", local_resp, hits).astype(jnp.bfloat16)
    flat_plane = per_plane.reshape(batch, classes * local_planes)
    planes_here = classes * local_planes
    share = width // lax.axis_size("img")
    square_pairs = jnp.repeat(ctf_square, 2, axis=1)
    summed = lax.psum_scatter(
        jnp.concatenate(
            [contract_first(weighted, flat_plane), contract_first(square_pairs, flat_plane)], axis=1
        ),
        "img",
        scatter_dimension=0,
        tiled=True,
    )
    numerator = summed[:, :planes_here]
    weight_sum = summed[:, planes_here:]
    updated = numerator / (weight_sum + 1.0)
    return jnp.transpose(updated).reshape(classes, local_planes, share)


def solution(mesh):
    return jax.shard_map(
        shards,
        mesh=mesh,
        in_specs=(
            P("img", None),
            P(None, "slab", None),
            P("img", None, None),
            P("img", None),
            P("img"),
            P(),
        ),
        out_specs=P(None, "slab", "img"),
        check_vma=False,
    )
```

profile of v0, /device:TPU:64, one launch (start us, length us, event | category | flops | bytes accessed | tf_op | source)
XLA Modules:
  0.0 655.7 jit_solution(16767141017079133494)
XLA Ops:
  6.6 0.6 convert_reduce_fusion
  7.3 3.9 multiply_convert_fusion.1
  11.2 6.9 %copy.33 = f32[64,16384]{0,1:T(8,128)} copy(f32[64,16384]{1,0:T(8,128)} %get-tuple-element.10) | data formatting | bytes 8388608 | tf_op jit(solution)/shard_map/dot_general | solution.py:38
  18.1 8.4 %copy.32 = bf16[64,32768]{0,1:T(8,128)(2,1)} copy(bf16[64,32768]{1,0:T(8,128)(2,1)} %param.6) | data formatting | bytes 8388608 | tf_op args[0]
  26.5 6.0 convert_multiply_fusion
  32.4 37.3 %copy.34 = f32[2,32,32768]{1,0,2:T(2,128)} copy(f32[2,32,32768]{2,1,0:T(8,128)} %convert_multiply_fusion) | data formatting | bytes 16777216 | tf_op jit(solution)/shard_map/mul | solution.py:45
  69.8 37.1 %mul.74 = f32[64,16384,2]{0,2,1:T(2,128)} reshape(f32[2,32,32768]{1,0,2:T(2,128)} %copy.34) | data formatting | bytes 16777216 | tf_op jit(solution)/shard_map/mul | solution.py:45
  106.9 3.2 copy.37
  110.1 73.2 %reduce_sum.28 = bf16[64,16384]{0,1:T(8,128)(2,1)} reduce(f32[64,16384,2]{0,2,1:T(2,128)} %mul.74, f32[]{:T(128)} %constant.64.clone.1), dimensions={2}, to_apply=%region_1.2 | reduce | flops 1048576 | bytes 10485764 | tf_op jit(solution)/shard_map/reduce_sum | solution.py:45
  183.2 9.6 %broadcast_in_dim.11 = f32[64,16384,2]{0,2,1:T(2,128)} broadcast(f32[64,16384]{0,1:T(8,128)} %copy.33), dimensions={0,1} | broadcast | bytes 12582912 | tf_op jit(solution)/shard_map/broadcast_in_dim | solution.py:41
  192.8 0.3 copy-done.3
  193.2 10.8 %convolution_multiply_fusion = f32[64,64]{1,0:T(8,128)S(1)} fusion(bf16[64,32768]{1,0:T(8,128)(2,1)S(1)} %bitcast.33, f32[64,32768]{0,1:T(8,128)} %bitcast.30, bf16[64,32768]{0,1:T(8,128)(2,1)} %copy.32), kind=kOutput, calls=%fused_computation.14 | convolution fusion | flops 274731008 | bytes 16793600 | tf_op jit(solution)/shard_map/dot_general | solution.py:27
  204.0 3.1 fusion.4
  207.2 15.6 %all_gather.3 = f32[64,2,128]{0,1,2:T(2,128)S(1)} all-gather(f32[64,2,32]{0,1,2:T(2,128)S(1)} %copy.36), channel_id=1, replica_groups=mesh['img'=64,'slab'=4] {'slab'}, dimensions={2}, use_global_device_ids=true | all-gather | bytes 81920 | tf_op jit(solution)/shard_map/all_gather | solution.py:53
  223.0 74.9 %gather_fusion = f32[8192]{0:T(1024)S(1)} fusion(f32[64,2,128]{0,1,2:T(2,128)S(1)} %all_gather.3, s32[8192]{0:T(1024)S(1)} %reshape.75), kind=kCustom, calls=%fused_computation | custom fusion | bytes 163840 | tf_op jit(solution)/shard_map/jit(take_along_axis)/gather | solution.py:54
  298.0 0.9 fusion.25
  299.0 1.0 fusion.23
  300.2 0.7 fusion.3
  300.9 11.3 %fusion.24 = f32[32768,64]{0,1:T(8,128)S(1)} fusion(bf16[64,64]{0,1:T(8,128)(2,1)S(1)} %bitcast.34, f32[64,32768]{0,1:T(8,128)} %bitcast.31, bf16[64,32768]{0,1:T(8,128)(2,1)} %copy.32), kind=kOutput, calls=%fused_computation.45 | convolution fusion | flops 274726912 | bytes 20979712 | tf_op jit(solution)/shard_map/dot_general | solution.py:21
  312.3 5.6 broadcast_in_dim.15
  317.8 6.4 fusion.27
  324.2 6.1 pad_maximum_fusion
  330.4 316.8 %reduce-scatter.2.cloned.1.call-done = f32[512,128]{0,1:T(8,128)} async-done(((f32[32768,128]{0,1:T(8,128)}), f32[512,128]{0,1:T(8,128)}) %reduce-scatter.2.cloned.1.call-update) | async-done | bytes 262160 | tf_op jit(solution)/shard_map/reduce_scatter | solution.py:67
  647.2 1.6 fusion.8
  (25 shorter events, 0.9 us)
Async XLA Ops:
  6.5 0.8 copy-start
  6.5 640.7 %reduce-scatter.2.cloned.1.call-start = ((), (), s32[]{:S(2)}) async-start(), calls=%async_computation.1 | async-start | bytes 17039360 | tf_op jit(solution)/shard_map/reduce_scatter | solution.py:67
  183.2 9.9 %copy-start.3 = (bf16[2,32,32768]{2,1,0:T(8,128)(2,1)S(1)}, bf16[2,32,32768]{2,1,0:T(8,128)(2,1)}, u32[]{:S(2)}) copy-start(bf16[2,32,32768]{2,1,0:T(8,128)(2,1)} %param.7) | copy-start | bytes 12582916
  204.0 18.9 %copy-start.4 = (s32[64,2,64]{2,1,0:T(2,128)S(1)}, s32[64,2,64]{2,1,0:T(2,128)}, u32[]{:S(2)}) copy-start(s32[64,2,64]{2,1,0:T(2,128)} %param.8) | copy-start | bytes 98308
  223.0 75.0 %copy-start.6 = (f32[2]{0:T(128)S(1)}, f32[2]{0:T(128)}, u32[]{:S(2)}) copy-start(f32[2]{0:T(128)} %param.11) | copy-start | bytes 28
  223.0 75.0 %copy-start.5 = (f32[64]{0:T(128)S(1)}, f32[64]{0:T(128)}, u32[]{:S(2)}) copy-start(f32[64]{0:T(128)} %param.10) | copy-start | bytes 772
  300.9 11.3 %copy-start.2 = (bf16[64,16384]{0,1:T(8,128)(2,1)S(1)}, bf16[64,16384]{0,1:T(8,128)(2,1)}, u32[]{:S(2)}) copy-start(bf16[64,16384]{0,1:T(8,128)(2,1)} %copy.37) | copy-start | bytes 6291460
  330.4 318.5 %copy-start.1 = (f32[64,64]{1,0:T(8,128)S(1)}, f32[64,64]{1,0:T(8,128)}, u32[]{:S(2)}) copy-start(f32[64,64]{1,0:T(8,128)} %param.9) | copy-start | bytes 49156
Sparse Core Ops, SparseCore 0:
  330.5 316.6 reduce-scatter.1
where the time goes:
time: 658 us; the launch traced here: 656 us
  waiting for transfers between devices  317 us (48%)
  local copies, waits for them, and re-layouts  184 us (28%)
  other arithmetic  89.7 us (14%)
  matrix products  36.2 us (6%)
  blocking collectives  15.6 us (2%)
  between operations  13.5 us (2%)
    reduce_scatter x1, waiting for transfers between devices, shards(): lax.psum_scatter(jnp.concatenate([contract_first(weighted, flat_plane), c...  317 us
    gather x3, local copies, waits for them, and re-layouts, shards(): picked = jnp.take_along_axis(table, orientations, axis=2)  75.1 us
    mul x2, local copies, waits for them, and re-layouts, shards(): power = jnp.sum(spread * spread, axis=2).astype(jnp.bfloat16)  74.5 us
    reduce_sum x1, other arithmetic, shards(): power = jnp.sum(spread * spread, axis=2).astype(jnp.bfloat16)  73.2 us
    dot_general x2, matrix products, contract_first(): lax.dot_general(left, right, (((0,), (0,)), ((), ())), preferred_element_...  17.7 us
    all_gather x1, blocking collectives, shards(): table = lax.all_gather(local_table, 'slab', axis=2, tiled=True)  15.6 us
    dot_general x2, matrix products, contract_last(): lax.dot_general(left, right, (((1,), (1,)), ((), ())), preferred_element_...  13.9 us
  transfers between devices with their start and end apart: 1, of which 1 were waited for; matrix products, arithmetic and copies ran while one was open for 0% of the time, Pallas kernels for 0%

commit v1 on v0

--- a/solution.py
+++ b/solution.py
@@ -50,7 +50,8 @@
     relative = orientations - offset
     inside = (relative >= 0) & (relative < local_planes)
     prior = jnp.log(class_weight)[None, :, None]
-    table = lax.all_gather(local_table, "slab", axis=2, tiled=True)
+    sent = jnp.stack([local_table] * lax.axis_size("slab"))
+    table = jnp.concatenate(lax.all_to_all(sent, "slab", 0, 0), axis=2)
     picked = jnp.take_along_axis(table, orientations, axis=2)
     scores = prior + inv_noise[:, None, None] * picked
     peak = jnp.max(scores, axis=(1, 2), keepdims=True)

time: 658 us -> 648 us (0.985)
  blocking collectives: 15.6 us -> 0 us
  starting transfers between devices: 0.01 us -> 8.11 us
    all_gather x1 -> x0, blocking collectives: 15.6 us -> none  [shards(): table = lax.all_gather(local_table, 'slab', axis=2, tiled=True)]
    all_to_all x0 -> x1, starting transfers between devices: none -> 8.11 us  [shards(): table = jnp.concatenate(lax.all_to_all(sent, 'slab', 0, 0), axis=2)]
    gather x3, local copies, waits for them, and re-layouts: 75.1 us -> 68.4 us  [shards(): picked = jnp.take_along_axis(table, orientations, axis=2)]
  transfers between devices with their start and end apart: 1 -> 2, of which waited for: 1 -> 2; matrix products, arithmetic and copies ran while one was open for 0% -> 1% of each run, Pallas kernels for 0% -> 0%
where the time goes in v1:
time: 648 us; the launch traced here: 646 us
  waiting for transfers between devices  319 us (49%)
  local copies, waits for them, and re-layouts  179 us (28%)
  other arithmetic  90.5 us (14%)
  matrix products  36.2 us (6%)
  between operations  13.5 us (2%)
  starting transfers between devices  8.11 us (1%)
    reduce_scatter x1, waiting for transfers between devices, shards(): lax.psum_scatter(jnp.concatenate([contract_first(weighted, flat_plane), c...  317 us
    mul x2, local copies, waits for them, and re-layouts, shards(): power = jnp.sum(spread * spread, axis=2).astype(jnp.bfloat16)  74.5 us
    reduce_sum x1, other arithmetic, shards(): power = jnp.sum(spread * spread, axis=2).astype(jnp.bfloat16)  73.1 us
    gather x3, local copies, waits for them, and re-layouts, shards(): picked = jnp.take_along_axis(table, orientations, axis=2)  68.4 us
    dot_general x2, matrix products, contract_first(): lax.dot_general(left, right, (((0,), (0,)), ((), ())), preferred_element_...  17.7 us
    dot_general x2, matrix products, contract_last(): lax.dot_general(left, right, (((1,), (1,)), ((), ())), preferred_element_...  13.9 us
  transfers between devices with their start and end apart: 2, of which 2 were waited for; matrix products, arithmetic and copies ran while one was open for 1% of the time, Pallas kernels for 0%

profile of v1, /device:TPU:64, one launch (start us, length us, event | category | flops | bytes accessed | tf_op | source)
XLA Modules:
  0.0 645.8 jit_solution(16199360637496724657)
XLA Ops:
  7.3 3.9 multiply_convert_fusion.1
  11.2 6.9 %copy.31 = f32[64,16384]{0,1:T(8,128)} copy(f32[64,16384]{1,0:T(8,128)} %get-tuple-element.10) | data formatting | bytes 8388608 | tf_op jit(solution)/shard_map/dot_general | solution.py:38
  18.1 8.4 %copy.30 = bf16[64,32768]{0,1:T(8,128)(2,1)} copy(bf16[64,32768]{1,0:T(8,128)(2,1)} %param.6) | data formatting | bytes 8388608 | tf_op args[0]
  26.5 6.0 convert_multiply_fusion
  32.4 37.3 %copy.32 = f32[2,32,32768]{1,0,2:T(2,128)} copy(f32[2,32,32768]{2,1,0:T(8,128)} %convert_multiply_fusion) | data formatting | bytes 16777216 | tf_op jit(solution)/shard_map/mul | solution.py:45
  69.8 37.1 %mul.74 = f32[64,16384,2]{0,2,1:T(2,128)} reshape(f32[2,32,32768]{1,0,2:T(2,128)} %copy.32) | data formatting | bytes 16777216 | tf_op jit(solution)/shard_map/mul | solution.py:45
  106.9 73.1 %reduce_sum.28 = bf16[64,16384]{0,1:T(8,128)(2,1)} reduce(f32[64,16384,2]{0,2,1:T(2,128)} %mul.74, f32[]{:T(128)} %constant.64.clone.1), dimensions={2}, to_apply=%region_1.2 | reduce | flops 1048576 | bytes 10485764 | tf_op jit(solution)/shard_map/reduce_sum | solution.py:45
  180.0 9.6 %broadcast_in_dim.11 = f32[64,16384,2]{0,2,1:T(2,128)} broadcast(f32[64,16384]{0,1:T(8,128)} %copy.31), dimensions={0,1} | broadcast | bytes 12582912 | tf_op jit(solution)/shard_map/broadcast_in_dim | solution.py:41
  189.9 10.8 %convolution_multiply_fusion = f32[64,64]{1,0:T(8,128)S(1)} fusion(bf16[64,32768]{1,0:T(8,128)(2,1)S(1)} %bitcast.41, f32[64,32768]{0,1:T(8,128)} %bitcast.38, bf16[64,32768]{0,1:T(8,128)(2,1)} %copy.30), kind=kOutput, calls=%fused_computation.14 | convolution fusion | flops 274731008 | bytes 16793600 | tf_op jit(solution)/shard_map/dot_general | solution.py:27
  200.8 3.1 fusion.4
  204.0 0.8 reshape.94
  204.7 8.1 %all-to-all-start = ((f32[4,1,4096]{2,1,0:T(1,128)}), f32[4,1,4096]{2,1,0:T(1,128)S(1)}, u32[]{:S(2)}, u32[]{:S(2)}) async-start(f32[4,1,4096]{2,1,0:T(1,128)} %reshape.94), calls=%async_computation | async-start | bytes 131072 | tf_op jit(solution)/shard_map/all_to_all | solution.py:54
  212.9 3.4 copy.35
  216.5 2.2 all-to-all-done
  219.1 0.8 reduce
  220.1 68.2 %gather_fusion = f32[8192]{0:T(1024)S(1)} fusion(f32[64,2,128]{0,2,1:T(8,128)S(1)} %bitcast.37, s32[8192]{0:T(1024)S(1)} %reshape.81), kind=kCustom, calls=%fused_computation | custom fusion | bytes 163840 | tf_op jit(solution)/shard_map/jit(take_along_axis)/gather | solution.py:55
  288.4 0.9 fusion.25
  289.4 1.0 fusion.23
  291.3 11.3 %fusion.24 = f32[32768,64]{0,1:T(8,128)S(1)} fusion(bf16[64,64]{0,1:T(8,128)(2,1)S(1)} %bitcast.42, f32[64,32768]{0,1:T(8,128)} %bitcast.39, bf16[64,32768]{0,1:T(8,128)(2,1)} %copy.30), kind=kOutput, calls=%fused_computation.45 | convolution fusion | flops 274726912 | bytes 20979712 | tf_op jit(solution)/shard_map/dot_general | solution.py:21
  302.7 5.6 broadcast_in_dim.15
  308.2 6.4 fusion.27
  314.6 6.1 pad_maximum_fusion
  320.8 316.5 %reduce-scatter.2.cloned.1.call-done = f32[512,128]{0,1:T(8,128)} async-done(((f32[32768,128]{0,1:T(8,128)}), f32[512,128]{0,1:T(8,128)}) %reduce-scatter.2.cloned.1.call-update) | async-done | bytes 262160 | tf_op jit(solution)/shard_map/reduce_scatter | solution.py:68
  637.3 1.6 fusion.8
  (32 shorter events, 3.1 us)
Async XLA Ops:
  6.5 0.8 copy-start
  180.0 9.9 %copy-start.3 = (bf16[2,32,32768]{2,1,0:T(8,128)(2,1)S(1)}, bf16[2,32,32768]{2,1,0:T(8,128)(2,1)}, u32[]{:S(2)}) copy-start(bf16[2,32,32768]{2,1,0:T(8,128)(2,1)} %param.7) | copy-start | bytes 12582916
  200.8 12.1 %copy-start.4 = (s32[64,2,64]{2,1,0:T(2,128)S(1)}, s32[64,2,64]{2,1,0:T(2,128)}, u32[]{:S(2)}) copy-start(s32[64,2,64]{2,1,0:T(2,128)} %param.8) | copy-start | bytes 98308
  203.9 12.6 %copy-start.6 = (f32[2]{0:T(128)S(1)}, f32[2]{0:T(128)}, u32[]{:S(2)}) copy-start(f32[2]{0:T(128)} %param.11) | copy-start | bytes 28
  204.7 13.9 %all-to-all-start = ((f32[4,1,4096]{2,1,0:T(1,128)}), f32[4,1,4096]{2,1,0:T(1,128)S(1)}, u32[]{:S(2)}, u32[]{:S(2)}) async-start(f32[4,1,4096]{2,1,0:T(1,128)} %reshape.94), calls=%async_computation | async-start | bytes 131072 | tf_op jit(solution)/shard_map/all_to_all | solution.py:54
  212.8 424.4 %reduce-scatter.2.cloned.1.call-start = ((), (), s32[]{:S(2)}) async-start(), calls=%async_computation.2 | async-start | bytes 17039360 | tf_op jit(solution)/shard_map/reduce_scatter | solution.py:68
  220.1 68.3 %copy-start.5 = (f32[64]{0:T(128)S(1)}, f32[64]{0:T(128)}, u32[]{:S(2)}) copy-start(f32[64]{0:T(128)} %param.10) | copy-start | bytes 772
  291.3 11.3 %copy-start.2 = (bf16[64,16384]{0,1:T(8,128)(2,1)S(1)}, bf16[64,16384]{0,1:T(8,128)(2,1)}, u32[]{:S(2)}) copy-start(bf16[64,16384]{0,1:T(8,128)(2,1)} %copy.35) | copy-start | bytes 6291460
  320.8 318.2 %copy-start.1 = (f32[64,64]{1,0:T(8,128)S(1)}, f32[64,64]{1,0:T(8,128)}, u32[]{:S(2)}) copy-start(f32[64,64]{1,0:T(8,128)} %param.9) | copy-start | bytes 49156
Sparse Core Ops, SparseCore 0:
  320.9 316.3 reduce-scatter.1
